TPU v7x, 512 devices: a whole 4x4x16 slice. The times are simulated.
512 devices in a mesh: branch: 8 (over y_lo, x), sky: 64 (over z, y_hi, core).
Axes of the slice: x: 4, y: 4 (y_hi: 2, y_lo: 2; y = y_hi * 2 + y_lo), z: 16, core: 2. Of those that a mesh axis runs over, the one named last changes fastest.
Arguments:
- sky_maps: bfloat16 [8, 64, 16384], P('branch', None, 'sky'), may hold values from -6 to 6
- footprint: int32 [8, 16384], P('branch', 'sky'), may hold values 0 or 1
- neighbours: int32 [9, 16384], P(None, 'sky'), may hold values from -1 to 16383, as said below
- enc_weight: bfloat16 [8, 6, 9, 64, 64], P('branch'), may hold values from -0.1875 to 0.1875
- join_weight: bfloat16 [256, 512], P(None, 'branch'), may hold values from -0.25 to 0.25
- dec_weight: bfloat16 [9, 256, 256], P(None, 'branch'), may hold values from -0.125 to 0.125
- cotangent: bfloat16 [256, 16384], P('branch', 'sky'), may hold values from -6 to 6
Outputs:
- map_grads: bfloat16 [8, 64, 16384], P('branch', None, 'sky')
- weight_grads: float32 [8, 6, 9, 64, 64], P('branch')
Inputs may be any that keep to these rules, and one draw needn't show every extreme that they name: `neighbours`: slot 4 of each row is the row itself; every other entry is -1 or a row index that differs from the row's own by at most 256.
All inputs are finite; a program needn't handle non-finite values. No bound on the sum of `footprint` on one device may be relied on, other than what follows from the above.
Results may differ from a plain program's by a relative error of at most 0.017.
Values may be sent and summed in bfloat16 or wider, within the bound.
No kernel may reach another device: no remote copies, remote signals or barrier semaphores. Data moves between devices by JAX's collectives and lax.ppermute only.
A program may use at most 64 MiB of HBM per device.

v0:
```python
import math
import jax
import jax.numpy as jnp
from jax import lax
from jax.sharding import PartitionSpec as P


def from_behind(value, axis, by):
    peers = lax.axis_size(axis)
    pairs = [(i, i + by) for i in range(peers) if 0 <= i + by < peers]
    return lax.ppermute(value, axis, pairs)


def with_halo(cells, sides, width):
    for axis, dim in sides:
        count = lax.axis_size(axis)
        ends = count - 1
        head = lax.slice_in_dim(cells, 0, width, axis=dim)
        tail = lax.slice_in_dim(cells, cells.shape[dim] - width, cells.shape[dim], axis=dim)
        cells = jnp.concatenate(
            [
                lax.ppermute(tail, axis, [(i, (i + 1) % count) for i in range(ends)]),
                cells,
                lax.ppermute(head, axis, [((i + 1) % count, i) for i in range(ends)]),
            ],
            axis=dim,
        )
    return cells


def silu_slope(value):
    sigmoid = jax.nn.sigmoid(value)
    return sigmoid * (1.0 + value * (1.0 - sigmoid))


def flat_taps(weight):
    return jnp.transpose(weight, (1, 2, 0)).reshape(weight.shape[1], -1)


def pick_columns(padded, position, present):
    channels = padded.shape[0]
    picked = jnp.take(padded, position.reshape(-1), axis=1).reshape(channels, 9, -1)
    return jnp.where(present[None], picked, jnp.zeros((), padded.dtype))


def spread_columns(contrib, position, present, channels, total_span):
    contrib = jnp.where(present[None], contrib.reshape(channels, 9, -1), 0.0)
    target = jnp.zeros((channels, total_span), jnp.float32)
    return target.at[:, position.reshape(-1)].add(contrib.reshape(channels, -1))


def fold_rims(padded, row_count):
    lower = from_behind(padded[:, :row_count].astype(jnp.bfloat16), "sky", -1).astype(jnp.float32)
    upper = from_behind(padded[:, 2 * row_count :].astype(jnp.bfloat16), "sky", 1).astype(
        jnp.float32
    )
    return padded[:, row_count : 2 * row_count] + lower + upper


def fold_unit_rims(padded, row_count):
    lower = from_behind(padded[:, :row_count].astype(jnp.bfloat16), "sky", -1).astype(jnp.float32)
    upper = from_behind(padded[:, 2 * row_count :].astype(jnp.bfloat16), "sky", 1).astype(
        jnp.float32
    )
    return padded[:, row_count : 2 * row_count] + lower + upper


def per_device(sky_maps, footprint, neighbours, enc_weight, join_weight, dec_weight, cotangent):
    row_count = sky_maps.shape[2]
    channels = sky_maps.shape[1]
    own_start = lax.axis_index("sky") * row_count
    first_row = own_start - row_count
    present = neighbours >= 0
    position = jnp.where(present, neighbours - first_row, 0)
    retained = footprint[0].astype(jnp.float32)[None, :]
    weights = enc_weight[0]
    depth = weights.shape[0]
    hidden = sky_maps[0]
    padded_list = []
    pre_list = []
    for layer_index in range(depth):
        padded = with_halo(hidden, (("sky", 1),), row_count)
        picked = pick_columns(padded, position, present)
        preact = jnp.dot(
            flat_taps(weights[layer_index]),
            picked.reshape(-1, row_count),
            preferred_element_type=jnp.float32,
        )
        hidden = (retained * (hidden.astype(jnp.float32) + jax.nn.silu(preact))).astype(
            jnp.bfloat16
        )
        padded_list.append(padded)
        pre_list.append(preact)
    partial_sum = jnp.dot(join_weight, hidden, preferred_element_type=jnp.float32)
    unit_share = lax.psum_scatter(
        partial_sum.astype(jnp.bfloat16), "branch", scatter_dimension=0, tiled=True
    ).astype(jnp.float32)
    slope_share = silu_slope(unit_share).astype(jnp.bfloat16)
    full_width = dec_weight.shape[2]
    dec_terms = lax.dot_general(
        flat_taps(dec_weight),
        cotangent,
        (((0,), (0,)), ((), ())),
        preferred_element_type=jnp.float32,
    )
    unit_pad = spread_columns(dec_terms, position, present, full_width, 3 * row_count)
    summed = lax.psum(fold_unit_rims(unit_pad, row_count), "branch")
    all_slopes = lax.all_gather(slope_share, "branch", axis=0, tiled=True)
    unit_grad = (summed * all_slopes.astype(jnp.float32)).astype(jnp.bfloat16)
    gradient = lax.dot_general(
        join_weight, unit_grad, (((0,), (0,)), ((), ())), preferred_element_type=jnp.float32
    )
    normalizer = 1.0 / math.sqrt(row_count * lax.axis_size("sky"))
    layer_grads = [None] * depth
    for layer_index in reversed(range(depth)):
        masked = retained * gradient
        act_grad = (masked * silu_slope(pre_list[layer_index])).astype(jnp.bfloat16)
        picked = pick_columns(padded_list[layer_index], position, present).reshape(-1, row_count)
        tap_grads = lax.dot_general(
            act_grad, picked, (((1,), (1,)), ((), ())), preferred_element_type=jnp.float32
        )
        layer_grads[layer_index] = jnp.transpose(
            tap_grads.reshape(channels, channels, 9), (2, 0, 1)
        )
        spread = lax.dot_general(
            flat_taps(weights[layer_index]),
            act_grad,
            (((0,), (0,)), ((), ())),
            preferred_element_type=jnp.float32,
        )
        gradient = masked + fold_rims(
            spread_columns(spread, position, present, channels, 3 * row_count), row_count
        )
    summed_weights = lax.psum(jnp.stack(layer_grads), "sky") * normalizer
    return (gradient.astype(jnp.bfloat16)[None], summed_weights[None])


def solution(mesh):
    in_specs = (
        P("branch", None, "sky"),
        P("branch", "sky"),
        P(None, "sky"),
        P("branch", None, None, None, None),
        P(None, "branch"),
        P(None, "branch", None),
        P("branch", "sky"),
    )
    out_specs = (P("branch", None, "sky"), P("branch", None, None, None, None))
    return jax.shard_map(
        per_device, mesh=mesh, in_specs=in_specs, out_specs=out_specs, check_vma=False
    )
```

profile of v0, /device:TPU:1, one launch (start us, length us, event | category | flops | bytes accessed | tf_op | source)
XLA Modules:
  0.0 955.9 jit_solution(9312221840940899464)
XLA Ops:
  7.2 6.2 collective-permute-start.2
  21.3 4.7 gather_fusion
  37.6 4.7 gather_fusion.1
  65.2 5.2 collective-permute-done.9
  70.6 4.7 gather_fusion.3
  82.9 14.1 %scatter_custom_fusion = f32[256,768]{0,1:T(8,128)S(1)} fusion(s32[2304]{0:T(1024)S(1)} %fusion.94, f32[2304,256]{1,0:T(8,128)} %bitcast.220, f32[]{:T(128)} %constant.17.clone.1), kind=kCustom, calls=%fused_computation.80 | custom fusion | flops 589824 | bytes 786944 | tf_op jit(solution)/shard_map/scatter-add | solution.py:49
  105.9 5.8 collective-permute-start.12
  116.3 5.1 collective-permute-start.1
  133.1 48.7 %reduce-scatter.4.cloned.1.call-done = bf16[32,256]{1,0:T(8,128)(2,1)} async-done(((bf16[256,256]{1,0:T(8,128)(2,1)}), bf16[32,256]{1,0:T(8,128)(2,1)}) %reduce-scatter.4.cloned.1.call-update) | async-done | bytes 16400 | tf_op jit(solution)/shard_map/reduce_scatter | solution.py:95
  182.6 21.8 %all_gather.3 = bf16[256,256]{1,0:T(8,128)(2,1)S(1)} all-gather(bf16[32,256]{1,0:T(8,128)(2,1)S(1)} %fusion.83), channel_id=1, replica_groups=mesh['branch'=8,'sky'=64] {'branch'}, dimensions={0}, use_global_device_ids=true | all-gather | bytes 147456 | tf_op jit(solution)/shard_map/all_gather | solution.py:108
  204.5 69.8 %all-reduce.3.cloned.1.call-done = f32[256,256]{0,1:T(8,128)} async-done(((f32[256,256]{0,1:T(8,128)}), f32[256,256]{0,1:T(8,128)}) %all-reduce.3.cloned.1.call-update) | async-done | bytes 262160 | tf_op jit(solution)/shard_map/psum | solution.py:107
  276.8 16.2 %scatter_custom_fusion.1 = f32[64,768]{0,1:T(8,128)S(1)} fusion(s32[2304]{0:T(1024)} %copy-done.40, f32[64,2304]{0,1:T(8,128)S(1)} %copy.134, f32[]{:T(128)} %constant.17.clone.1, pred[2304]{0:T(1024)(128)(4,1)S(1)} %broadcast_in_dim.154), kind=kCustom, calls=%fused_computation.31 | custom fusion | flops 294912 | bytes 789760 | tf_op jit(solution)/shard_map/scatter-add | solution.py:49
  293.1 7.5 collective-permute-start.14
  307.7 16.0 %scatter_custom_fusion.2 = f32[64,768]{0,1:T(8,128)S(1)} fusion(s32[2304]{0:T(1024)} %copy-done.40, f32[64,2304]{0,1:T(8,128)S(1)} %copy.138, f32[]{:T(128)} %constant.17.clone.1, pred[2304]{0:T(1024)(128)(4,1)S(1)} %broadcast_in_dim.154), kind=kCustom, calls=%fused_computation.29 | custom fusion | flops 294912 | bytes 789760 | tf_op jit(solution)/shard_map/scatter-add | solution.py:49
  325.9 5.9 collective-permute-start.17
  334.4 16.2 %scatter_custom_fusion.3 = f32[64,768]{0,1:T(8,128)S(1)} fusion(s32[2304]{0:T(1024)} %copy-done.40, f32[64,2304]{0,1:T(8,128)S(1)} %copy.142, f32[]{:T(128)} %constant.17.clone.1, pred[2304]{0:T(1024)(128)(4,1)S(1)} %broadcast_in_dim.154), kind=kCustom, calls=%fused_computation.27 | custom fusion | flops 294912 | bytes 789760 | tf_op jit(solution)/shard_map/scatter-add | solution.py:49
  352.6 5.3 collective-permute-start.19
  360.7 16.0 %scatter_custom_fusion.4 = f32[64,768]{0,1:T(8,128)S(1)} fusion(s32[2304]{0:T(1024)} %copy-done.40, f32[64,2304]{0,1:T(8,128)S(1)} %copy.146, f32[]{:T(128)} %constant.17.clone.1, pred[2304]{0:T(1024)(128)(4,1)S(1)} %broadcast_in_dim.154), kind=kCustom, calls=%fused_computation.25 | custom fusion | flops 294912 | bytes 789760 | tf_op jit(solution)/shard_map/scatter-add | solution.py:49
  378.9 5.7 collective-permute-start.21
  387.8 16.0 %scatter_custom_fusion.5 = f32[64,768]{0,1:T(8,128)S(1)} fusion(s32[2304]{0:T(1024)} %copy-done.40, f32[64,2304]{0,1:T(8,128)S(1)} %copy.150, f32[]{:T(128)} %constant.17.clone.1, pred[2304]{0:T(1024)(128)(4,1)S(1)} %broadcast_in_dim.154), kind=kCustom, calls=%fused_computation.23 | custom fusion | flops 294912 | bytes 789760 | tf_op jit(solution)/shard_map/scatter-add | solution.py:49
  406.0 5.6 collective-permute-start.23
  418.3 16.0 %scatter_custom_fusion.6 = f32[64,768]{0,1:T(8,128)S(1)} fusion(s32[2304]{0:T(1024)} %copy-done.40, f32[64,2304]{0,1:T(8,128)S(1)} %copy.154, f32[]{:T(128)} %constant.17.clone.1, pred[2304]{0:T(1024)(128)(4,1)S(1)} %broadcast_in_dim.154), kind=kCustom, calls=%fused_computation.21 | custom fusion | flops 294912 | bytes 789760 | tf_op jit(solution)/shard_map/scatter-add | solution.py:49
  436.4 5.7 collective-permute-start.25
  443.8 502.4 %all-reduce.5.cloned.1.call-done = f32[6,9,64,64]{3,2,1,0:T(8,128)} async-done(((f32[6,9,64,64]{3,2,1,0:T(8,128)}), f32[6,9,64,64]{3,2,1,0:T(8,128)}) %all-reduce.5.cloned.1.call-update) | async-done | bytes 884752 | tf_op jit(solution)/shard_map/psum | solution.py:134
  (248 shorter events, 115.1 us)
Async XLA Ops:
  7.2 174.7 %reduce-scatter.4.cloned.1.call-start = ((), (), s32[]{:S(2)}) async-start(), calls=%async_computation.3 | async-start | bytes 147456 | tf_op jit(solution)/shard_map/reduce_scatter | solution.py:95
  7.2 12.3 %collective-permute-start.2 = (bf16[64,256]{1,0:T(8,128)(2,1)}, bf16[64,256]{1,0:T(8,128)(2,1)S(1)}, u32[]{:S(2)}, u32[]{:S(2)}) collective-permute-start(bf16[64,256]{1,0:T(8,128)(2,1)} %bitcast.241), channel_id=1, source_target_pairs={{0,1},{1,2},{2,3},{3,4},{4,5},{5,6},{6,7},{7,8},{8,9},{9,10},{10,1... | collective-permute-start | bytes 98312 | tf_op jit(solution)/shard_map/ppermute | solution.py:22
  13.4 7.0 collective-permute-start.3
  30.7 6.7 collective-permute-start.5
  46.6 7.1 collective-permute-start.7
  63.0 7.4 collective-permute-start.9
  78.5 19.3 %collective-permute-start.10 = (bf16[64,256]{1,0:T(8,128)(2,1)S(1)}, bf16[64,256]{1,0:T(8,128)(2,1)S(1)}, u32[]{:S(2)}, u32[]{:S(2)}) collective-permute-start(bf16[64,256]{1,0:T(8,128)(2,1)S(1)} %get-tuple-element.35), channel_id=1, source_target_pairs={{0,1},{1,2},{2,3},{3,4},{4,5},{5,6},{6,7},{7,8},{8,9},{9,10},{10,1... | collective-permute-start | bytes 98312 | tf_op jit(solution)/shard_map/ppermute | solution.py:22
  80.4 17.4 %collective-permute-start.11 = (bf16[64,256]{1,0:T(8,128)(2,1)S(1)}, bf16[64,256]{1,0:T(8,128)(2,1)S(1)}, u32[]{:S(2)}, u32[]{:S(2)}) collective-permute-start(bf16[64,256]{1,0:T(8,128)(2,1)S(1)} %get-tuple-element.35), channel_id=1, source_target_pairs={{1,0},{2,1},{3,2},{4,3},{5,4},{6,5},{7,6},{8,7},{9,8},{10,9},{11,1... | collective-permute-start | bytes 98312 | tf_op jit(solution)/shard_map/ppermute | solution.py:24
  105.9 15.5 %collective-permute-start.12 = (bf16[64,256]{1,0:T(8,128)(2,1)S(1)}, bf16[64,256]{1,0:T(8,128)(2,1)S(1)}, u32[]{:S(2)}, u32[]{:S(2)}) collective-permute-start(bf16[64,256]{1,0:T(8,128)(2,1)S(1)} %get-tuple-element.37), channel_id=1, source_target_pairs={{0,1},{1,2},{2,3},{3,4},{4,5},{5,6},{6,7},{7,8},{8,9},{9,10},{10,1... | collective-permute-start | bytes 98312 | tf_op jit(solution)/shard_map/ppermute | solution.py:22
  111.7 9.7 %collective-permute-start.13 = (bf16[64,256]{1,0:T(8,128)(2,1)S(1)}, bf16[64,256]{1,0:T(8,128)(2,1)S(1)}, u32[]{:S(2)}, u32[]{:S(2)}) collective-permute-start(bf16[64,256]{1,0:T(8,128)(2,1)S(1)} %get-tuple-element.37), channel_id=1, source_target_pairs={{1,0},{2,1},{3,2},{4,3},{5,4},{6,5},{7,6},{8,7},{9,8},{10,9},{11,1... | collective-permute-start | bytes 98312 | tf_op jit(solution)/shard_map/ppermute | solution.py:24
  114.3 17.0 %collective-permute-start = (bf16[256,256]{0,1:T(8,128)(2,1)}, bf16[256,256]{0,1:T(8,128)(2,1)}, u32[]{:S(2)}, u32[]{:S(2)}) collective-permute-start(bf16[256,256]{0,1:T(8,128)(2,1)} %get-tuple-element.15), channel_id=1, source_target_pairs={{1,0},{2,1},{3,2},{4,3},{5,4},{6,5},{7,6},{8,7},{9,8},{10,9},{11,1... | collective-permute-start | bytes 393224 | tf_op jit(solution)/shard_map/ppermute | solution.py:11
  116.3 15.1 %collective-permute-start.1 = (bf16[256,256]{0,1:T(8,128)(2,1)}, bf16[256,256]{0,1:T(8,128)(2,1)}, u32[]{:S(2)}, u32[]{:S(2)}) collective-permute-start(bf16[256,256]{0,1:T(8,128)(2,1)} %get-tuple-element.16), channel_id=1, source_target_pairs={{0,1},{1,2},{2,3},{3,4},{4,5},{5,6},{6,7},{7,8},{8,9},{9,10},{10,1... | collective-permute-start | bytes 393224 | tf_op jit(solution)/shard_map/ppermute | solution.py:11
  130.0 144.2 %all-reduce.3.cloned.1.call-start = ((), (), s32[]{:S(2)}) async-start(), calls=%async_computation.1 | async-start | bytes 524288 | tf_op jit(solution)/shard_map/psum | solution.py:107
  133.1 813.1 %all-reduce.5.cloned.1.call-start = ((), (), s32[]{:S(2)}) async-start(), calls=%async_computation.2 | async-start | bytes 3538944 | tf_op jit(solution)/shard_map/psum | solution.py:134
  293.1 12.1 %collective-permute-start.14 = (bf16[64,256]{1,0:T(8,128)(2,1)S(1)}, bf16[64,256]{1,0:T(8,128)(2,1)S(1)}, u32[]{:S(2)}, u32[]{:S(2)}) collective-permute-start(bf16[64,256]{1,0:T(8,128)(2,1)S(1)} %get-tuple-element.27), channel_id=1, source_target_pairs={{1,0},{2,1},{3,2},{4,3},{5,4},{6,5},{7,6},{8,7},{9,8},{10,9},{11,1... | collective-permute-start | bytes 98312 | tf_op jit(solution)/shard_map/ppermute | solution.py:11
  324.0 9.1 collective-permute-start.16
  325.9 7.2 collective-permute-start.17
  350.7 7.6 collective-permute-start.18
  377.0 8.9 collective-permute-start.20
  378.9 7.0 collective-permute-start.21
  404.0 7.6 collective-permute-start.22
  406.0 6.4 collective-permute-start.23
  434.5 7.7 collective-permute-start.24
  436.4 6.7 collective-permute-start.25
  (46 other events, 444.8 us)
Sparse Core Ops, SparseCore 0:
  130.2 51.6 reduce-scatter.3
  185.6 88.6 all-reduce.2
  417.3 528.8 all-reduce.4
where the time goes:
time: 966 us; the launch traced here: 956 us
  waiting for transfers between devices  636 us (66%)
  other arithmetic  129 us (13%)
  starting transfers between devices  91.8 us (10%)
  local copies, waits for them, and re-layouts  47.1 us (5%)
  blocking collectives  21.8 us (2%)
  between operations  15.5 us (2%)
  matrix products  14.2 us (1%)
    psum x1, waiting for transfers between devices, per_device(): summed_weights = lax.psum(jnp.stack(layer_grads), 'sky') * normalizer  502 us
    scatter-add x7, other arithmetic, spread_columns(): return target.at[:, position.reshape(-1)].add(contrib.reshape(channels, -1))  110 us
    psum x1, waiting for transfers between devices, per_device(): summed = lax.psum(fold_unit_rims(unit_pad, row_count), 'branch')  69.8 us
    ppermute x14, starting transfers between devices, from_behind(): return lax.ppermute(value, axis, pairs)  56.7 us
    reduce_scatter x1, waiting for transfers between devices, per_device(): lax.psum_scatter(partial_sum.astype(jnp.bfloat16), 'branch', scatter_dime...  48.7 us
    gather x6, local copies, waits for them, and re-layouts, pick_columns(): jnp.take(padded, position.reshape(-1), axis=1).reshape(channels, 9, -1)  28 us
    all_gather x1, blocking collectives, per_device(): all_slopes = lax.all_gather(slope_share, 'branch', axis=0, tiled=True)  21.8 us
    ppermute x6, starting transfers between devices, with_halo(): lax.ppermute(tail, axis, [(i, (i + 1) % count) for i in range(ends)])  20.3 us
  transfers between devices with their start and end apart: 29, of which 11 were waited for; matrix products, arithmetic and copies ran while one was open for 6% of the time, Pallas kernels for 0%

commit v1 on v0

--- a/solution.py
+++ b/solution.py
@@ -104,7 +104,7 @@
         preferred_element_type=jnp.float32,
     )
     unit_pad = spread_columns(dec_terms, position, present, full_width, 3 * row_count)
-    summed = lax.psum(fold_unit_rims(unit_pad, row_count), "branch")
+    summed = jnp.sum(lax.all_gather(fold_unit_rims(unit_pad, row_count), "branch"), axis=0)
     all_slopes = lax.all_gather(slope_share, "branch", axis=0, tiled=True)
     unit_grad = (summed * all_slopes.astype(jnp.float32)).astype(jnp.bfloat16)
     gradient = lax.dot_general(

time: 966 us -> 923 us (0.955)
  waiting for transfers between devices: 636 us -> 596 us
    psum x1 -> x0, waiting for transfers between devices: 69.8 us -> none  [per_device(): summed = lax.psum(fold_unit_rims(unit_pad, row_count), 'branch')]
    all_gather x0 -> x1, waiting for transfers between devices: none -> 28.4 us  [per_device(): lax.all_gather(fold_unit_rims(unit_pad, row_count), 'branch')]
  transfers between devices with their start and end apart: 29 -> 29, of which waited for: 11 -> 13; matrix products, arithmetic and copies ran while one was open for 6% -> 6% of each run, Pallas kernels for 0% -> 0%
where the time goes in v1:
time: 923 us; the launch traced here: 914 us
  waiting for transfers between devices  596 us (65%)
  other arithmetic  128 us (14%)
  starting transfers between devices  92.4 us (10%)
  local copies, waits for them, and re-layouts  47.4 us (5%)
  blocking collectives  21.8 us (2%)
  between operations  15.4 us (2%)
  matrix products  12.3 us (1%)
    psum x1, waiting for transfers between devices, per_device(): summed_weights = lax.psum(jnp.stack(layer_grads), 'sky') * normalizer  503 us
    scatter-add x7, other arithmetic, spread_columns(): return target.at[:, position.reshape(-1)].add(contrib.reshape(channels, -1))  110 us
    ppermute x14, starting transfers between devices, from_behind(): return lax.ppermute(value, axis, pairs)  57.3 us
    reduce_scatter x1, waiting for transfers between devices, per_device(): lax.psum_scatter(partial_sum.astype(jnp.bfloat16), 'branch', scatter_dime...  48.7 us
    all_gather x1, waiting for transfers between devices, per_device(): lax.all_gather(fold_unit_rims(unit_pad, row_count), 'branch')  28.4 us
    gather x6, local copies, waits for them, and re-layouts, pick_columns(): jnp.take(padded, position.reshape(-1), axis=1).reshape(channels, 9, -1)  28 us
    all_gather x1, blocking collectives, per_device(): all_slopes = lax.all_gather(slope_share, 'branch', axis=0, tiled=True)  21.8 us
    ppermute x6, starting transfers between devices, with_halo(): lax.ppermute(tail, axis, [(i, (i + 1) % count) for i in range(ends)])  20.3 us
  transfers between devices with their start and end apart: 29, of which 13 were waited for; matrix products, arithmetic and copies ran while one was open for 6% of the time, Pallas kernels for 0%

profile of v1, /device:TPU:1, one launch (start us, length us, event | category | flops | bytes accessed | tf_op | source)
XLA Modules:
  0.0 913.7 jit_solution(11667547817191933423)
XLA Ops:
  7.2 6.2 collective-permute-start.2
  21.3 4.7 gather_fusion
  37.6 4.7 gather_fusion.1
  53.8 4.7 gather_fusion.2
  65.2 5.2 collective-permute-done.9
  82.0 14.1 %scatter_custom_fusion = f32[256,768]{0,1:T(8,128)S(1)} fusion(s32[2304]{0:T(1024)S(1)} %fusion.94, f32[2304,256]{1,0:T(8,128)} %bitcast.225, f32[]{:T(128)} %constant.17.clone.1), kind=kCustom, calls=%fused_computation.81 | custom fusion | flops 589824 | bytes 786944 | tf_op jit(solution)/shard_map/scatter-add | solution.py:49
  105.0 5.8 collective-permute-start.12
  115.3 5.1 collective-permute-start.1
  132.2 48.7 %reduce-scatter.4.cloned.1.call-done = bf16[32,256]{1,0:T(8,128)(2,1)} async-done(((bf16[256,256]{1,0:T(8,128)(2,1)}), bf16[32,256]{1,0:T(8,128)(2,1)}) %reduce-scatter.4.cloned.1.call-update) | async-done | bytes 16400 | tf_op jit(solution)/shard_map/reduce_scatter | solution.py:95
  181.6 21.8 %all_gather.11 = bf16[256,256]{1,0:T(8,128)(2,1)S(1)} all-gather(bf16[32,256]{1,0:T(8,128)(2,1)S(1)} %fusion.83), channel_id=1, replica_groups=mesh['branch'=8,'sky'=64] {'branch'}, dimensions={0}, use_global_device_ids=true | all-gather | bytes 147456 | tf_op jit(solution)/shard_map/all_gather | solution.py:108
  203.6 28.4 %all-gather.3.cloned.1.call-done = f32[2048,256]{0,1:T(8,128)} async-done(((f32[256,256]{0,1:T(8,128)}), f32[2048,256]{0,1:T(8,128)}) %all-gather.3.cloned.1.call-update) | async-done | bytes 2097168 | tf_op jit(solution)/shard_map/all_gather | solution.py:107
  236.7 15.9 %scatter_custom_fusion.1 = f32[64,768]{0,1:T(8,128)S(1)} fusion(s32[2304]{0:T(1024)S(1)} %fusion.94, f32[64,2304]{0,1:T(8,128)S(1)} %copy.173, f32[]{:T(128)} %constant.17.clone.1, pred[2304]{0:T(1024)(128)(4,1)S(1)} %broadcast_in_dim.154), kind=kCustom, calls=%fused_computation.32 | custom fusion | flops 294912 | bytes 1380352 | tf_op jit(solution)/shard_map/scatter-add | solution.py:49
  252.8 8.0 collective-permute-start.14
  267.0 15.9 %scatter_custom_fusion.2 = f32[64,768]{0,1:T(8,128)S(1)} fusion(s32[2304]{0:T(1024)S(1)} %fusion.94, f32[64,2304]{0,1:T(8,128)S(1)} %copy.177, f32[]{:T(128)} %constant.17.clone.1, pred[2304]{0:T(1024)(128)(4,1)S(1)} %broadcast_in_dim.154), kind=kCustom, calls=%fused_computation.30 | custom fusion | flops 294912 | bytes 1380352 | tf_op jit(solution)/shard_map/scatter-add | solution.py:49
  285.1 5.7 collective-permute-start.17
  293.1 16.2 %scatter_custom_fusion.3 = f32[64,768]{0,1:T(8,128)S(1)} fusion(s32[2304]{0:T(1024)} %copy-done.41, f32[64,2304]{0,1:T(8,128)S(1)} %copy.181, f32[]{:T(128)} %constant.17.clone.1, pred[2304]{0:T(1024)(128)(4,1)S(1)} %broadcast_in_dim.154), kind=kCustom, calls=%fused_computation.28 | custom fusion | flops 294912 | bytes 789760 | tf_op jit(solution)/shard_map/scatter-add | solution.py:49
  311.3 5.7 collective-permute-start.19
  319.9 16.2 %scatter_custom_fusion.4 = f32[64,768]{0,1:T(8,128)S(1)} fusion(s32[2304]{0:T(1024)} %copy-done.41, f32[64,2304]{0,1:T(8,128)S(1)} %copy.185, f32[]{:T(128)} %constant.17.clone.1, pred[2304]{0:T(1024)(128)(4,1)S(1)} %broadcast_in_dim.154), kind=kCustom, calls=%fused_computation.26 | custom fusion | flops 294912 | bytes 789760 | tf_op jit(solution)/shard_map/scatter-add | solution.py:49
  338.2 5.9 collective-permute-start.21
  345.9 16.0 %scatter_custom_fusion.5 = f32[64,768]{0,1:T(8,128)S(1)} fusion(s32[2304]{0:T(1024)} %copy-done.41, f32[64,2304]{0,1:T(8,128)S(1)} %copy.189, f32[]{:T(128)} %constant.17.clone.1, pred[2304]{0:T(1024)(128)(4,1)S(1)} %broadcast_in_dim.154), kind=kCustom, calls=%fused_computation.24 | custom fusion | flops 294912 | bytes 789760 | tf_op jit(solution)/shard_map/scatter-add | solution.py:49
  364.0 5.9 collective-permute-start.23
  375.9 16.0 %scatter_custom_fusion.6 = f32[64,768]{0,1:T(8,128)S(1)} fusion(s32[2304]{0:T(1024)} %copy-done.41, f32[64,2304]{0,1:T(8,128)S(1)} %copy.193, f32[]{:T(128)} %constant.17.clone.1, pred[2304]{0:T(1024)(128)(4,1)S(1)} %broadcast_in_dim.154), kind=kCustom, calls=%fused_computation.22 | custom fusion | flops 294912 | bytes 789760 | tf_op jit(solution)/shard_map/scatter-add | solution.py:49
  394.1 5.7 collective-permute-start.25
  401.5 502.6 %all-reduce.2.cloned.1.call-done = f32[6,9,64,64]{3,2,1,0:T(8,128)} async-done(((f32[6,9,64,64]{3,2,1,0:T(8,128)}), f32[6,9,64,64]{3,2,1,0:T(8,128)}) %all-reduce.2.cloned.1.call-update) | async-done | bytes 884752 | tf_op jit(solution)/shard_map/psum | solution.py:134
  (252 shorter events, 113.1 us)
Async XLA Ops:
  7.2 173.7 %reduce-scatter.4.cloned.1.call-start = ((), (), s32[]{:S(2)}) async-start(), calls=%async_computation.3 | async-start | bytes 147456 | tf_op jit(solution)/shard_map/reduce_scatter | solution.py:95
  7.2 12.3 %collective-permute-start.2 = (bf16[64,256]{1,0:T(8,128)(2,1)}, bf16[64,256]{1,0:T(8,128)(2,1)S(1)}, u32[]{:S(2)}, u32[]{:S(2)}) collective-permute-start(bf16[64,256]{1,0:T(8,128)(2,1)} %bitcast.247), channel_id=1, source_target_pairs={{0,1},{1,2},{2,3},{3,4},{4,5},{5,6},{6,7},{7,8},{8,9},{9,10},{10,1... | collective-permute-start | bytes 98312 | tf_op jit(solution)/shard_map/ppermute | solution.py:22
  13.4 7.0 collective-permute-start.3
  46.6 7.1 collective-permute-start.7
  63.0 7.4 collective-permute-start.9
  77.6 19.3 %collective-permute-start.10 = (bf16[64,256]{1,0:T(8,128)(2,1)S(1)}, bf16[64,256]{1,0:T(8,128)(2,1)S(1)}, u32[]{:S(2)}, u32[]{:S(2)}) collective-permute-start(bf16[64,256]{1,0:T(8,128)(2,1)S(1)} %get-tuple-element.35), channel_id=1, source_target_pairs={{0,1},{1,2},{2,3},{3,4},{4,5},{5,6},{6,7},{7,8},{8,9},{9,10},{10,1... | collective-permute-start | bytes 98312 | tf_op jit(solution)/shard_map/ppermute | solution.py:22
  79.5 17.3 %collective-permute-start.11 = (bf16[64,256]{1,0:T(8,128)(2,1)S(1)}, bf16[64,256]{1,0:T(8,128)(2,1)S(1)}, u32[]{:S(2)}, u32[]{:S(2)}) collective-permute-start(bf16[64,256]{1,0:T(8,128)(2,1)S(1)} %get-tuple-element.35), channel_id=1, source_target_pairs={{1,0},{2,1},{3,2},{4,3},{5,4},{6,5},{7,6},{8,7},{9,8},{10,9},{11,1... | collective-permute-start | bytes 98312 | tf_op jit(solution)/shard_map/ppermute | solution.py:24
  105.0 15.5 %collective-permute-start.12 = (bf16[64,256]{1,0:T(8,128)(2,1)S(1)}, bf16[64,256]{1,0:T(8,128)(2,1)S(1)}, u32[]{:S(2)}, u32[]{:S(2)}) collective-permute-start(bf16[64,256]{1,0:T(8,128)(2,1)S(1)} %get-tuple-element.37), channel_id=1, source_target_pairs={{0,1},{1,2},{2,3},{3,4},{4,5},{5,6},{6,7},{7,8},{8,9},{9,10},{10,1... | collective-permute-start | bytes 98312 | tf_op jit(solution)/shard_map/ppermute | solution.py:22
  110.8 9.7 %collective-permute-start.13 = (bf16[64,256]{1,0:T(8,128)(2,1)S(1)}, bf16[64,256]{1,0:T(8,128)(2,1)S(1)}, u32[]{:S(2)}, u32[]{:S(2)}) collective-permute-start(bf16[64,256]{1,0:T(8,128)(2,1)S(1)} %get-tuple-element.37), channel_id=1, source_target_pairs={{1,0},{2,1},{3,2},{4,3},{5,4},{6,5},{7,6},{8,7},{9,8},{10,9},{11,1... | collective-permute-start | bytes 98312 | tf_op jit(solution)/shard_map/ppermute | solution.py:24
  113.4 15.7 %collective-permute-start = (bf16[256,256]{0,1:T(8,128)(2,1)}, bf16[256,256]{0,1:T(8,128)(2,1)}, u32[]{:S(2)}, u32[]{:S(2)}) collective-permute-start(bf16[256,256]{0,1:T(8,128)(2,1)} %get-tuple-element.15), channel_id=1, source_target_pairs={{1,0},{2,1},{3,2},{4,3},{5,4},{6,5},{7,6},{8,7},{9,8},{10,9},{11,1... | collective-permute-start | bytes 393224 | tf_op jit(solution)/shard_map/ppermute | solution.py:11
  115.3 13.8 %collective-permute-start.1 = (bf16[256,256]{0,1:T(8,128)(2,1)}, bf16[256,256]{0,1:T(8,128)(2,1)}, u32[]{:S(2)}, u32[]{:S(2)}) collective-permute-start(bf16[256,256]{0,1:T(8,128)(2,1)} %get-tuple-element.16), channel_id=1, source_target_pairs={{0,1},{1,2},{2,3},{3,4},{4,5},{5,6},{6,7},{7,8},{8,9},{9,10},{10,1... | collective-permute-start | bytes 393224 | tf_op jit(solution)/shard_map/ppermute | solution.py:11
  129.1 102.9 %all-gather.3.cloned.1.call-start = ((), (), s32[]{:S(2)}) async-start(), calls=%async_computation.2 | async-start | bytes 2359296 | tf_op jit(solution)/shard_map/all_gather | solution.py:107
  130.9 773.1 %all-reduce.2.cloned.1.call-start = ((), (), s32[]{:S(2)}) async-start(), calls=%async_computation.1 | async-start | bytes 3538944 | tf_op jit(solution)/shard_map/psum | solution.py:134
  252.8 12.0 %collective-permute-start.14 = (bf16[64,256]{1,0:T(8,128)(2,1)S(1)}, bf16[64,256]{1,0:T(8,128)(2,1)S(1)}, u32[]{:S(2)}, u32[]{:S(2)}) collective-permute-start(bf16[64,256]{1,0:T(8,128)(2,1)S(1)} %get-tuple-element.27), channel_id=1, source_target_pairs={{1,0},{2,1},{3,2},{4,3},{5,4},{6,5},{7,6},{8,7},{9,8},{10,9},{11,1... | collective-permute-start | bytes 98312 | tf_op jit(solution)/shard_map/ppermute | solution.py:11
  283.2 8.0 collective-permute-start.16
  285.1 6.7 collective-permute-start.17
  309.4 8.0 collective-permute-start.18
  311.3 6.7 collective-permute-start.19
  336.3 8.2 collective-permute-start.20
  338.2 6.8 collective-permute-start.21
  362.1 7.8 collective-permute-start.22
  364.0 6.9 collective-permute-start.23
  392.2 7.7 collective-permute-start.24
  394.1 6.7 collective-permute-start.25
  (47 other events, 641.8 us)
Sparse Core Ops, SparseCore 0:
  129.2 51.6 reduce-scatter.3
  183.8 48.1 all-gather.2
  374.9 529.0 all-reduce.1
